TPU v7x, 32 devices: a whole 2x2x4 slice. The times are simulated.
32 devices in a mesh: seq: 8 (over z, y), tensor: 4 (over x, core).
Axes of the slice: x: 2, y: 2, z: 4, core: 2. Of those that a mesh axis runs over, the one named last changes fastest.
Arguments:
- queries: bfloat16 [768, 4096], P('seq', 'tensor'), may hold values from -96 to 96
- keys: bfloat16 [768, 1024], P('seq', 'tensor'), may hold values from -96 to 96
- values: bfloat16 [768, 1024], P('seq', 'tensor'), may hold values from -6 to 6
- out_weight: bfloat16 [4096, 4096], P('tensor'), may hold values from -0.09375 to 0.09375
- doc_lengths: int32 [16], replicated, may hold values from 1 to 192, 768 in all
- stretch_place: int32 [16], replicated, may hold values from 0 to 15, each once
Outputs:
- output: bfloat16 [768, 4096], P('seq', 'tensor')
Inputs may be any that keep to these rules, and one draw needn't show every extreme that they name: `stretch_place`: each stored block number appears once. `doc_lengths`: the lengths sum to 768; the longest is exactly 192.
All inputs are finite; a program needn't handle non-finite values.
Results may differ from a plain program's by a relative error of at most 0.015.
Values may be sent and summed in bfloat16 or wider, within the bound.
A program may use at most 64 MiB of HBM per device.

v0:
```python
import math

import jax
import jax.numpy as jnp
from jax import lax
from jax.sharding import PartitionSpec as P

HD = 128


rope_base = 500000.0


def for_sending(value):
    return jax.tree.map(lambda a: a.astype(jnp.bfloat16) if a.dtype == jnp.float32 else a, value)


def from_partner(block, axis, apart):
    count = lax.axis_size(axis)
    route = []
    for low in range(count):
        high = low | 1 << apart
        if high != low and high < count:
            route += [(low, high), (high, low)]
    return lax.ppermute(block, axis, route)


def seq_positions(first, count, stretch_place, block_rows):
    row_index = first + jnp.arange(count, dtype=jnp.int32)
    return stretch_place[row_index // block_rows] * block_rows + row_index % block_rows


def documents(positions, doc_lengths):
    ends = jnp.cumsum(doc_lengths)
    return jnp.sum((ends[None, :] <= positions[:, None]).astype(jnp.int32), axis=1)


def rotary(heads_in, positions):
    width = heads_in.shape[-1]
    half = width // 2
    freqs = rope_base ** (-(2.0 / width) * jnp.arange(half, dtype=jnp.float32))
    angles = positions.astype(jnp.float32)[:, None] * freqs[None, :]
    cosine = jnp.cos(angles)[:, None, :]
    sine = jnp.sin(angles)[:, None, :]
    floats = heads_in.astype(jnp.float32)
    first_half = floats[..., :half]
    second_half = floats[..., half:]
    rotated = jnp.concatenate(
        [first_half * cosine - second_half * sine, second_half * cosine + first_half * sine],
        axis=-1,
    )
    return rotated.astype(jnp.bfloat16)


def key_block_rows(count):
    for candidate in (512, 384, 256, 192, 128, 96, 64, 48, 32, 16, 8):
        if candidate <= count and count % candidate == 0:
            return candidate
    return count


def body(queries, keys, values, out_weight, doc_lengths, stretch_place):
    tok_rows = queries.shape[0]
    block_rows = tok_rows // 2
    head_size = HD
    kv_local = keys.shape[1] // head_size
    q_local = queries.shape[1] // head_size
    group = q_local // kv_local
    device = lax.axis_index("seq")
    own_start = device * tok_rows
    positions = seq_positions(own_start, tok_rows, stretch_place, block_rows)
    document = documents(positions, doc_lengths)
    q_rot = rotary(queries.reshape(tok_rows, q_local, head_size), positions).reshape(
        tok_rows, kv_local, group, head_size
    )
    k_rot = rotary(keys.reshape(tok_rows, kv_local, head_size), positions)
    value_heads = values.reshape(tok_rows, kv_local, head_size)
    scale = 1.0 / math.sqrt(head_size)

    def attend_block(state, key_piece, value_piece, start):
        count = key_piece.shape[0]
        key_positions = seq_positions(start, count, stretch_place, block_rows)
        key_document = documents(key_positions, doc_lengths)
        allowed = (key_positions[None, :] <= positions[:, None]) & (
            key_document[None, :] == document[:, None]
        )
        run_max, run_total, accum = state
        scores = (
            jnp.einsum("tkgd,nkd->kgtn", q_rot, key_piece, preferred_element_type=jnp.float32)
            * scale
        )
        scores = jnp.where(allowed[None, None], scores, -1e30)
        new_max = jnp.maximum(run_max, jnp.max(scores, axis=-1))
        weights = jnp.where(allowed[None, None], jnp.exp(scores - new_max[..., None]), 0.0)
        factor = jnp.exp(run_max - new_max)
        new_total = run_total * factor + jnp.sum(weights, axis=-1)
        update = jnp.einsum(
            "kgtn,nkd->tkgd",
            weights.astype(jnp.bfloat16),
            value_piece,
            preferred_element_type=jnp.float32,
        )
        new_accum = accum * jnp.transpose(factor, (2, 0, 1))[..., None] + update
        return (new_max, new_total, new_accum)

    def attend(state, piece, start):
        key_piece, value_piece = piece
        count = key_piece.shape[0]
        step_rows = key_block_rows(count)
        if step_rows == count:
            return attend_block(state, key_piece, value_piece, start)
        steps_total = count // step_rows
        key_blocks = key_piece.reshape(steps_total, step_rows, kv_local, head_size)
        value_blocks = value_piece.reshape(steps_total, step_rows, kv_local, head_size)

        def one_step(carry, inputs):
            key_block, value_block, offset = inputs
            return (attend_block(carry, key_block, value_block, start + offset * step_rows), None)

        offsets = jnp.arange(steps_total, dtype=jnp.int32)
        result, unused = lax.scan(one_step, state, (key_blocks, value_blocks, offsets))
        return result

    initial = (
        jnp.full((kv_local, group, tok_rows), -1e30, jnp.float32),
        jnp.zeros((kv_local, group, tok_rows), jnp.float32),
        jnp.zeros((tok_rows, kv_local, group, head_size), jnp.float32),
    )
    state = attend(initial, (k_rot, value_heads), own_start)
    holding = (k_rot, value_heads)
    levels = lax.axis_size("seq").bit_length() - 1
    for level in range(levels):
        received = jax.tree.map(
            lambda part, own: part.astype(own.dtype),
            from_partner(for_sending(holding), "seq", level),
            holding,
        )
        span = 2**level
        partner = jnp.bitwise_xor(device, span)
        partner_first = partner // span * span
        state = attend(state, received, partner_first * tok_rows)
        if level + 1 < levels:
            upper = device // span % 2 == 1
            holding = jax.tree.map(
                lambda own_part, their_part: jnp.where(
                    upper,
                    jnp.concatenate([their_part, own_part], 0),
                    jnp.concatenate([own_part, their_part], 0),
                ),
                holding,
                received,
            )
    run_max, run_total, accum = state
    attended = (
        (accum / jnp.transpose(run_total, (2, 0, 1))[..., None])
        .astype(jnp.bfloat16)
        .reshape(tok_rows, q_local * head_size)
    )
    partial_rows = jnp.dot(attended, out_weight, preferred_element_type=jnp.float32)
    return lax.psum_scatter(
        partial_rows.astype(jnp.bfloat16), "tensor", scatter_dimension=1, tiled=True
    )


def solution(mesh):
    in_specs = (
        P("seq", "tensor"),
        P("seq", "tensor"),
        P("seq", "tensor"),
        P("tensor", None),
        P(),
        P(),
    )
    out_specs = P("seq", "tensor")
    return jax.shard_map(body, mesh=mesh, in_specs=in_specs, out_specs=out_specs, check_vma=False)
```

profile of v0, /device:TPU:0, one launch (start us, length us, event | category | flops | bytes accessed | tf_op | source)
XLA Modules:
  0.0 107.7 jit_solution(9048978571494118042)
XLA Ops:
  6.5 0.0 copy-start
  6.5 0.0 copy-start.1
  6.5 0.0 reduce-scatter.2.cloned.1.call-start
  6.6 1.9 %fusion.80 = (s32[1]{0:T(128)}, s32[1]{0:T(128)}, s32[1]{0:T(128)}, s32[1]{0:T(128)}, s32[1]{0:T(128)}, /*index=5*/s32[1]{0:T(128)}, s32[1]{0:T(128)}, s32[1]{0:...) fusion(s32[16]{0:T(128)} %param.11), kind=kLoop, calls=%fused_computation.195 | loop fusion | bytes 128 | tf_op jit(solution)/shard_map/gather | solution.py:30
  8.5 0.8 reshape.601
  9.4 0.2 fusion.79
  9.5 10.0 %fusion.76 = (f32[96]{0:T(128)S(1)}, s32[96]{0:T(128)S(1)}, s32[96]{0:T(128)S(1)}) fusion(s32[]{:T(128)S(6)} %mul.226, s32[]{:T(128)} %bitcast.24, s32[]{:T(128)} %bitcast.23, s32[]{:T(128)} %bitcast.22, s32[]{:T(128)} %bitcast.21, s32[]{:T(128)} %bitcast.20, s32[]{:T(128)} %bitcast.19, s32[]{:T(128)} %bitcast.18, s32[]{:T(128)} %bitcast.17, s32[]{:T(128)} %bitcast.15, ...), kind=kLoop, calls=%fused_computation.192 | loop fusion | flops 9888 | bytes 1224 | tf_op jit(solution)/shard_map/convert_element_type | solution.py:42
  19.5 0.2 multiply_cosine_fusion
  19.8 0.1 pad_maximum_fusion.1
  19.9 3.1 %collective-permute-start = (bf16[96,2,128]{2,0,1:T(8,128)(2,1)S(1)}, bf16[96,2,128]{2,0,1:T(8,128)(2,1)S(1)}, u32[]{:S(2)}, u32[]{:S(2)}) collective-permute-start(bf16[96,2,128]{2,0,1:T(8,128)(2,1)S(1)} %pad_maximum_fusion.1), channel_id=1, source_target_pairs={{0,4},{4,0},{8,12},{12,8},{16,20},{20,16},{24,28},{28,24},{1,5},{5... | collective-permute-start | bytes 147464 | tf_op jit(solution)/shard_map/ppermute | solution.py:25
  23.0 0.0 copy-done
  23.0 0.1 collective-permute-start.1
  23.1 4.4 %compare_select_fusion.8 = s32[192,1]{0,1:T(1,128)S(1)} fusion(s32[]{:T(128)} %bitcast.18, s32[]{:T(128)} %bitcast.19, s32[]{:T(128)} %bitcast.20, s32[]{:T(128)} %bitcast.21, s32[]{:T(128)} %bitcast.22, s32[]{:T(128)} %bitcast.24, s32[]{:T(128)} %bitcast.23, s32[]{:T(128)S(6)} %mul.253), kind=kLoop, calls=%fused_computation.124 | loop fusion | flops 4608 | bytes 800 | tf_op jit(solution)/shard_map/gather | solution.py:30
  27.6 4.4 %fusion.60 = s32[384]{0:T(512)S(1)} fusion(s32[]{:T(128)} %bitcast.18, s32[]{:T(128)} %bitcast.19, s32[]{:T(128)} %bitcast.20, s32[]{:T(128)} %bitcast.21, s32[]{:T(128)} %bitcast.22, s32[]{:T(128)} %bitcast.24, s32[]{:T(128)} %bitcast.23, s32[]{:T(128)S(6)} %mul.260), kind=kLoop, calls=%fused_computation.176 | loop fusion | flops 9216 | bytes 1568 | tf_op jit(solution)/shard_map/gather | solution.py:30
  32.2 0.0 copy-done.1
  32.2 0.0 copy-start.2
  32.2 0.1 copy.57
  32.3 0.2 fusion.78
  32.5 0.4 copy-done.2
  32.9 0.1 copy.26
  33.0 0.1 reduce
  33.1 5.6 %fusion.61 = s32[192]{0:T(256)S(1)} fusion(pred[192]{0:T(512)(128)(4,1)S(1)} %get-tuple-element.63, pred[192]{0:T(512)(128)(4,1)S(1)} %get-tuple-element.64, pred[192]{0:T(512)(128)(4,1)S(1)} %get-tuple-element.65, pred[192]{0:T(512)(128)(4,1)S(1)} %get-tuple-element.66, pred[192]{0:T(512)(128)(4,1)S(1)} %get-tuple-element.67, ...), kind=kLoop, calls=%fused_computation.177 | loop fusion | flops 3456 | bytes 3304 | tf_op jit(solution)/shard_map/add | solution.py:30
  38.7 0.1 convert_reduce_fusion.1
  38.8 5.6 %fusion.56 = s32[384]{0:T(512)S(1)} fusion(pred[384]{0:T(512)(128)(4,1)S(1)} %get-tuple-element.55, pred[384]{0:T(512)(128)(4,1)S(1)} %get-tuple-element.56, pred[384]{0:T(512)(128)(4,1)S(1)} %get-tuple-element.57, pred[384]{0:T(512)(128)(4,1)S(1)} %get-tuple-element.58, pred[384]{0:T(512)(128)(4,1)S(1)} %get-tuple-element.59, ...), kind=kLoop, calls=%fused_computation.134 | loop fusion | flops 6912 | bytes 6568 | tf_op jit(solution)/shard_map/add | solution.py:30
  44.5 0.1 convert_reduce_fusion
  44.5 0.1 convert_reduce_fusion.2
  44.6 0.1 compare_and_fusion.3
  44.8 0.1 compare_and_fusion
  44.9 0.2 subtract_convert_fusion
  45.0 0.1 pad_maximum_fusion
  45.2 0.3 fusion.84
  45.5 0.1 compare_and_fusion.1
  45.7 0.0 collective-permute-done
  45.7 0.1 maximum_select_fusion.2
  45.8 2.1 %collective-permute-start.2 = (bf16[192,2,128]{2,0,1:T(8,128)(2,1)S(1)}, bf16[192,2,128]{2,0,1:T(8,128)(2,1)S(1)}, u32[]{:S(2)}, u32[]{:S(2)}) collective-permute-start(bf16[192,2,128]{2,0,1:T(8,128)(2,1)S(1)} %maximum_select_fusion.2), channel_id=1, source_target_pairs={{0,8},{8,0},{4,12},{12,4},{16,24},{24,16},{20,28},{28,20},{1,9},{9... | collective-permute-start | bytes 294920 | tf_op jit(solution)/shard_map/ppermute | solution.py:25
  47.9 0.0 collective-permute-done.1
  47.9 0.1 collective-permute-start.3
  48.0 0.3 fusion.83
  48.3 3.1 %collective-permute-done.2 = bf16[192,2,128]{2,0,1:T(8,128)(2,1)S(1)} collective-permute-done((bf16[192,2,128]{2,0,1:T(8,128)(2,1)S(1)}, bf16[192,2,128]{2,0,1:T(8,128)(2,1)S(1)}, u32[]{:S(2)}, u32[]{:S(2)}) %collective-permute-start.2) | collective-permute-done | bytes 98336 | tf_op jit(solution)/shard_map/ppermute | solution.py:25
  51.4 0.1 maximum_select_fusion
  51.4 3.0 %collective-permute-start.4 = (bf16[384,2,128]{2,0,1:T(8,128)(2,1)S(1)}, bf16[384,2,128]{2,0,1:T(8,128)(2,1)S(1)}, u32[]{:S(2)}, u32[]{:S(2)}) collective-permute-start(bf16[384,2,128]{2,0,1:T(8,128)(2,1)S(1)} %maximum_select_fusion), channel_id=1, source_target_pairs={{0,16},{16,0},{4,20},{20,4},{8,24},{24,8},{12,28},{28,12},{1,17},{... | collective-permute-start | bytes 589832 | tf_op jit(solution)/shard_map/ppermute | solution.py:25
  54.4 0.0 collective-permute-done.3
  54.4 0.1 maximum_select_fusion.1
  54.5 2.0 %collective-permute-start.5 = (bf16[384,2,128]{2,0,1:T(8,128)(2,1)S(1)}, bf16[384,2,128]{2,0,1:T(8,128)(2,1)S(1)}, u32[]{:S(2)}, u32[]{:S(2)}) collective-permute-start(bf16[384,2,128]{2,0,1:T(8,128)(2,1)S(1)} %maximum_select_fusion.1), channel_id=1, source_target_pairs={{0,16},{16,0},{4,20},{20,4},{8,24},{24,8},{12,28},{28,12},{1,17},{... | collective-permute-start | bytes 589832 | tf_op jit(solution)/shard_map/ppermute | solution.py:25
  56.5 0.3 fusion.82
  56.8 10.5 %collective-permute-done.4 = bf16[384,2,128]{2,0,1:T(8,128)(2,1)S(1)} collective-permute-done((bf16[384,2,128]{2,0,1:T(8,128)(2,1)S(1)}, bf16[384,2,128]{2,0,1:T(8,128)(2,1)S(1)}, u32[]{:S(2)}, u32[]{:S(2)}) %collective-permute-start.4) | collective-permute-done | bytes 196640 | tf_op jit(solution)/shard_map/ppermute | solution.py:25
  67.4 0.4 fusion.81
  67.8 0.1 fusion.29
  67.9 0.1 fusion.31
  68.0 0.2 fusion.19
  68.2 0.4 fusion.17
  68.7 0.4 convolution_bitcast_fusion.1
  69.0 0.4 fusion.9
  69.4 0.1 collective-permute-done.5
  69.5 0.4 convolution_bitcast_fusion
  69.9 0.5 fusion.16
  70.3 0.1 copy.38
  70.5 0.1 reshape.600
  70.6 5.7 %convolution_convert_fusion = bf16[96,4096]{1,0:T(8,128)(2,1)} fusion(bf16[96,1024]{1,0:T(8,128)(2,1)S(1)} %reshape.600, bf16[1024,4096]{1,0:T(8,128)(2,1)} %param.9), kind=kOutput, calls=%fused_computation | convolution fusion | flops 805699584 | bytes 9371648 | tf_op jit(solution)/shard_map/dot_general | solution.py:159
  76.3 0.0 reduce-scatter.2.cloned.1.call-update
  76.3 24.5 %reduce-scatter.2.cloned.1.call-done = bf16[96,1024]{1,0:T(8,128)(2,1)} async-done(((bf16[96,4096]{1,0:T(8,128)(2,1)}), bf16[96,1024]{1,0:T(8,128)(2,1)}) %reduce-scatter.2.cloned.1.call-update) | async-done | bytes 196624 | tf_op jit(solution)/shard_map/reduce_scatter | solution.py:160
  (19 shorter events, 0.5 us)
Async XLA Ops:
  6.5 16.4 %copy-start = (bf16[96,256]{1,0:T(8,128)(2,1)S(1)}, bf16[96,256]{1,0:T(8,128)(2,1)}, u32[]{:S(2)}) copy-start(bf16[96,256]{1,0:T(8,128)(2,1)} %param.8) | copy-start | bytes 147460
  6.5 25.6 %copy-start.1 = (bf16[96,1024]{1,0:T(8,128)(2,1)S(1)}, bf16[96,1024]{1,0:T(8,128)(2,1)}, u32[]{:S(2)}) copy-start(bf16[96,1024]{1,0:T(8,128)(2,1)} %param.6) | copy-start | bytes 589828
  6.5 94.3 %reduce-scatter.2.cloned.1.call-start = ((), (), s32[]{:S(2)}) async-start(), calls=%async_computation.1 | async-start | bytes 983040 | tf_op jit(solution)/shard_map/reduce_scatter | solution.py:160
  19.9 25.8 %collective-permute-start = (bf16[96,2,128]{2,0,1:T(8,128)(2,1)S(1)}, bf16[96,2,128]{2,0,1:T(8,128)(2,1)S(1)}, u32[]{:S(2)}, u32[]{:S(2)}) collective-permute-start(bf16[96,2,128]{2,0,1:T(8,128)(2,1)S(1)} %pad_maximum_fusion.1), channel_id=1, source_target_pairs={{0,4},{4,0},{8,12},{12,8},{16,20},{20,16},{24,28},{28,24},{1,5},{5... | collective-permute-start | bytes 147464 | tf_op jit(solution)/shard_map/ppermute | solution.py:25
  23.0 24.9 %collective-permute-start.1 = (bf16[96,2,128]{2,0,1:T(8,128)(2,1)S(1)}, bf16[96,2,128]{2,0,1:T(8,128)(2,1)S(1)}, u32[]{:S(2)}, u32[]{:S(2)}) collective-permute-start(bf16[96,2,128]{2,0,1:T(8,128)(2,1)S(1)} %copy_bitcast_fusion), channel_id=1, source_target_pairs={{0,4},{4,0},{8,12},{12,8},{16,20},{20,16},{24,28},{28,24},{1,5},{5... | collective-permute-start | bytes 147464 | tf_op jit(solution)/shard_map/ppermute | solution.py:25
  32.2 0.7 copy-start.2
  45.8 5.6 %collective-permute-start.2 = (bf16[192,2,128]{2,0,1:T(8,128)(2,1)S(1)}, bf16[192,2,128]{2,0,1:T(8,128)(2,1)S(1)}, u32[]{:S(2)}, u32[]{:S(2)}) collective-permute-start(bf16[192,2,128]{2,0,1:T(8,128)(2,1)S(1)} %maximum_select_fusion.2), channel_id=1, source_target_pairs={{0,8},{8,0},{4,12},{12,4},{16,24},{24,16},{20,28},{28,20},{1,9},{9... | collective-permute-start | bytes 294920 | tf_op jit(solution)/shard_map/ppermute | solution.py:25
  47.9 6.5 %collective-permute-start.3 = (bf16[192,2,128]{2,0,1:T(8,128)(2,1)S(1)}, bf16[192,2,128]{2,0,1:T(8,128)(2,1)S(1)}, u32[]{:S(2)}, u32[]{:S(2)}) collective-permute-start(bf16[192,2,128]{2,0,1:T(8,128)(2,1)S(1)} %maximum_select_fusion.3), channel_id=1, source_target_pairs={{0,8},{8,0},{4,12},{12,4},{16,24},{24,16},{20,28},{28,20},{1,9},{9... | collective-permute-start | bytes 294920 | tf_op jit(solution)/shard_map/ppermute | solution.py:25
  51.4 15.9 %collective-permute-start.4 = (bf16[384,2,128]{2,0,1:T(8,128)(2,1)S(1)}, bf16[384,2,128]{2,0,1:T(8,128)(2,1)S(1)}, u32[]{:S(2)}, u32[]{:S(2)}) collective-permute-start(bf16[384,2,128]{2,0,1:T(8,128)(2,1)S(1)} %maximum_select_fusion), channel_id=1, source_target_pairs={{0,16},{16,0},{4,20},{20,4},{8,24},{24,8},{12,28},{28,12},{1,17},{... | collective-permute-start | bytes 589832 | tf_op jit(solution)/shard_map/ppermute | solution.py:25
  54.5 15.0 %collective-permute-start.5 = (bf16[384,2,128]{2,0,1:T(8,128)(2,1)S(1)}, bf16[384,2,128]{2,0,1:T(8,128)(2,1)S(1)}, u32[]{:S(2)}, u32[]{:S(2)}) collective-permute-start(bf16[384,2,128]{2,0,1:T(8,128)(2,1)S(1)} %maximum_select_fusion.1), channel_id=1, source_target_pairs={{0,16},{16,0},{4,20},{20,4},{8,24},{24,8},{12,28},{28,12},{1,17},{... | collective-permute-start | bytes 589832 | tf_op jit(solution)/shard_map/ppermute | solution.py:25
Sparse Core Ops, SparseCore 0:
  76.4 24.3 reduce-scatter.1
where the time goes:
time: 108 us
  waiting for transfers between devices  38.2 us (35%)
  other arithmetic  32.8 us (30%)
  between operations  13.7 us (13%)
  starting transfers between devices  10.4 us (10%)
  matrix products  8.65 us (8%)
  local copies, waits for them, and re-layouts  3.95 us (4%)
    reduce_scatter x1, waiting for transfers between devices, body(): lax.psum_scatter(partial_rows.astype(jnp.bfloat16), 'tensor', scatter_dim...  24.5 us
    ppermute x6, waiting for transfers between devices, from_partner(): return lax.ppermute(block, axis, route)  13.7 us
    add x2, other arithmetic, seq_positions(): stretch_place[row_index // block_rows] * block_rows + row_index % block_rows  11.2 us
    ppermute x6, starting transfers between devices, from_partner(): return lax.ppermute(block, axis, route)  10.4 us
    convert_element_type x1, other arithmetic, rotary(): angles = positions.astype(jnp.float32)[:, None] * freqs[None, :]  9.97 us
    gather x12, other arithmetic, seq_positions(): stretch_place[row_index // block_rows] * block_rows + row_index % block_rows  9.07 us
    dot_general x1, matrix products, body(): jnp.dot(attended, out_weight, preferred_element_type=jnp.float32)  5.72 us
  transfers between devices with their start and end apart: 7, of which 4 were waited for; matrix products, arithmetic and copies ran while one was open for 23% of the time, Pallas kernels for 0%

commit v1 on v0

v1 whole, which is shorter than its diff:
```python
import functools
import math

import jax
import jax.numpy as jnp
from jax import lax
from jax.experimental import pallas as pl
from jax.experimental.pallas import tpu as pltpu
from jax.sharding import PartitionSpec as P

HD = 128
ROPE_BASE = 500000.0
MASKED = -1e30
FLOOR = -5e29
F32 = jnp.float32
BF16 = jnp.bfloat16
MESH = pl.DeviceIdType.MESH
UNROLL_MOST = 8


def kernel(
    seq_count,
    tensor_count,
    pieces,
    lengths_ref,
    place_ref,
    q_hbm,
    k_hbm,
    v_hbm,
    w_hbm,
    out_ref,
    q_in,
    k_in,
    gk,
    gv,
    qs,
    w_buf,
    attended,
    run_max,
    run_total,
    accum,
    kept,
    send_core,
    recv_core,
    send_chip,
    recv_chip,
    load_sem,
    gather_send,
    gather_recv,
    core_send_sem,
    core_recv_sem,
    chip_send_sem,
    chip_recv_sem,
):
    rows = q_in.shape[0]
    half_rows = rows // 2
    kv_local = k_in.shape[1] // HD
    group = q_in.shape[1] // k_in.shape[1]
    wide = group * rows
    line = seq_count // 2
    chips = tensor_count // 2
    chunk = w_buf.shape[2]
    width = chunk // pieces

    me = lax.axis_index("seq")
    p, y = me // 2, me % 2
    t = lax.axis_index("tensor")
    a, c = t // 2, t % 2
    has_up, has_down = p < line - 1, p > 0
    beside = p * 2 + (1 - y)
    other_core = a * 2 + (1 - c)

    loads = [
        pltpu.make_async_copy(k_hbm, k_in, load_sem.at[0]),
        pltpu.make_async_copy(v_hbm, gv.at[me], load_sem.at[1]),
        pltpu.make_async_copy(q_hbm, q_in, load_sem.at[2]),
    ]
    for load in loads:
        load.start()

    barrier = pltpu.get_barrier_semaphore()

    def greet(where):
        pl.semaphore_signal(barrier, inc=1, device_id=where, device_id_type=MESH)

    greet({"seq": beside})
    greet({"tensor": other_core})
    for i in range(1, chips):
        greet({"tensor": (a + i) % chips * 2 + c})

    @pl.when(has_up)
    def _():
        greet({"seq": me + 2})

    @pl.when(has_down)
    def _():
        greet({"seq": me - 2})

    pl.semaphore_wait(
        barrier, 1 + chips + has_up.astype(jnp.int32) + has_down.astype(jnp.int32)
    )

    def gather_copy(way, block, kind, own=False):
        buf = gk if kind == 0 else gv
        src = v_hbm if own and kind == 1 else buf.at[block]
        target = (me + 2, me - 2, beside)[way]
        return pltpu.make_async_remote_copy(
            src_ref=src,
            dst_ref=buf.at[block],
            send_sem=gather_send.at[way, block // 2, kind],
            recv_sem=gather_recv.at[block, kind],
            device_id={"seq": target},
            device_id_type=MESH,
        )

    def send_own(kind):
        @pl.when(has_up)
        def _():
            gather_copy(0, me, kind, True).start()

        @pl.when(has_down)
        def _():
            gather_copy(1, me, kind, True).start()

        gather_copy(2, me, kind, True).start()

    def arrived(block, kind):
        gather_copy(2, block, kind).wait_recv()

    def forward(place, kind):
        block = place * 2 + y

        @pl.when((place < p) & has_up)
        def _():
            gather_copy(0, block, kind).start()

        @pl.when((place > p) & has_down)
        def _():
            gather_copy(1, block, kind).start()

        gather_copy(2, block, kind).start()

    send_own(1)

    def owner(slot):
        i = slot // 2 + 1
        return (a + i) % chips * 2 + jnp.where(slot % 2 == 0, 1 - c, c)

    weight_loads = []
    for slot in range(tensor_count):
        start = pl.multiple_of(owner(slot) * chunk, 128)
        weight_loads.append(
            pltpu.make_async_copy(
                w_hbm.at[:, pl.ds(start, chunk)], w_buf.at[slot], load_sem.at[3 + slot]
            )
        )

    base0 = place_ref[2 * me] * half_rows
    base1 = place_ref[2 * me + 1] * half_rows

    def positions(shape, axis):
        row = lax.broadcasted_iota(jnp.int32, shape, axis) % rows
        return jnp.where(row < half_rows, base0 + row, base1 + row - half_rows)

    lane = lax.broadcasted_iota(jnp.int32, (rows, HD), 1)
    freq = jnp.exp((lane % (HD // 2)).astype(F32) * (-2.0 / HD * math.log(ROPE_BASE)))
    angle = positions((rows, HD), 0).astype(F32) * freq
    cosine = jnp.cos(angle)
    sine = jnp.where(lane < HD // 2, -jnp.sin(angle), jnp.sin(angle))

    def rotate(block):
        floats = block.astype(F32)
        return (floats * cosine + pltpu.roll(floats, HD // 2, 1) * sine).astype(BF16)

    loads[0].wait()
    for h in range(kv_local):
        gk[me, :, h * HD : (h + 1) * HD] = rotate(k_in[:, h * HD : (h + 1) * HD])
    send_own(0)
    for load in weight_loads:
        load.start()

    loads[2].wait()
    for h in range(kv_local):
        for g in range(group):
            column = (h * group + g) * HD
            qs[h, g * rows : (g + 1) * rows, :] = rotate(q_in[:, column : column + HD])

    last = positions((1, wide), 1)
    first = jnp.zeros((1, wide), jnp.int32)
    end = jnp.int32(0)
    for i in range(lengths_ref.shape[0]):
        end = end + lengths_ref[i]
        first = jnp.maximum(first, jnp.where(end <= last, end, 0))

    run_max[...] = jnp.full_like(run_max, FLOOR)
    run_total[...] = jnp.zeros_like(run_total)
    accum[...] = jnp.zeros_like(accum)
    scale = math.log2(math.e) / math.sqrt(HD)

    def attend(block):
        row = lax.broadcasted_iota(jnp.int32, (half_rows, wide), 0)
        allowed = []
        for j in range(2):
            base = place_ref[2 * block + j] * half_rows
            allowed.append((row >= first - base) & (row <= last - base))
        for h in range(kv_local):
            key = gk[block, :, h * HD : (h + 1) * HD]
            value = gv[block, :, h * HD : (h + 1) * HD]
            scores = lax.dot_general(
                key, qs[h], (((1,), (1,)), ((), ())), preferred_element_type=F32
            )
            scores = jnp.concatenate(
                [
                    jnp.where(allowed[j], scores[j * half_rows : (j + 1) * half_rows], MASKED)
                    for j in range(2)
                ],
                axis=0,
            )
            old = run_max[h]
            new = jnp.maximum(old, jnp.max(scores, axis=0, keepdims=True))
            weights = jnp.exp2((scores - new) * scale)
            factor = jnp.exp2((old - new) * scale)
            run_max[h] = new
            run_total[h] = run_total[h] * factor + jnp.sum(weights, axis=0, keepdims=True)
            accum[h] = accum[h] * factor + lax.dot_general(
                value,
                weights.astype(BF16),
                (((0,), (0,)), ((), ())),
                preferred_element_type=F32,
            )

    loads[1].wait()
    attend(me)

    near = jnp.minimum(p, line - 1 - p)

    def nth_place(k):
        apart = (k + 1) // 2
        both = jnp.where(k % 2 == 1, p - apart, p + apart)
        single = jnp.where(p < line - 1 - p, p + (k - near), p - (k - near))
        return jnp.where(k <= 2 * near, both, single)

    def step(k):
        place = nth_place(k)
        for kind in (1, 0):
            arrived(place * 2 + y, kind)
            forward(place, kind)
        attend(place * 2 + y)
        across = nth_place(k - 1) * 2 + (1 - y)
        for kind in (1, 0):
            arrived(across, kind)
        attend(across)

    def repeat(low, high, body):
        if high - low < UNROLL_MOST:
            for k in range(low, high):
                body(jnp.int32(k))
        else:

            def one(k, carry):
                body(k)
                return carry

            lax.fori_loop(low, high, one, 0)

    repeat(1, line, step)
    across = nth_place(jnp.int32(line - 1)) * 2 + (1 - y)
    for kind in (1, 0):
        arrived(across, kind)
    attend(across)

    for h in range(kv_local):
        mixed = (accum[h] * (1.0 / run_total[h])).T.astype(BF16)
        for g in range(group):
            column = (h * group + g) * HD
            attended[:, column : column + HD] = mixed[g * rows : (g + 1) * rows]

    def partial_sum(slot, j):
        return jnp.dot(
            attended[...],
            w_buf[slot, :, j * width : (j + 1) * width],
            preferred_element_type=F32,
        )

    def core_copy(i, j):
        return pltpu.make_async_remote_copy(
            src_ref=send_core.at[i, j],
            dst_ref=recv_core.at[i, j],
            send_sem=core_send_sem.at[i, j],
            recv_sem=core_recv_sem.at[i, j],
            device_id={"tensor": other_core},
            device_id_type=MESH,
        )

    def chip_copy(i, j):
        return pltpu.make_async_remote_copy(
            src_ref=send_chip.at[i, j],
            dst_ref=recv_chip.at[i, j],
            send_sem=chip_send_sem.at[i, j],
            recv_sem=chip_recv_sem.at[i, j],
            device_id={"tensor": (a + i + 1) % chips * 2 + c},
            device_id_type=MESH,
        )

    def pass_on(i, j):
        core_copy(i, j).wait_recv()
        send_chip[i, j] = (kept[i, j] + recv_core[i, j].astype(F32)).astype(BF16)
        chip_copy(i, j).start()

    waiting = []
    for i in range(chips):
        for j in range(pieces):
            if j == 0:
                weight_loads[2 * i].wait()
            send_core[i, j] = partial_sum(2 * i, j).astype(BF16)
            core_copy(i, j).start()
            if j == 0:
                weight_loads[2 * i + 1].wait()
            kept[i, j] = partial_sum(2 * i + 1, j)
            if waiting:
                pass_on(*waiting.pop())
            if i < chips - 1:
                waiting.append((i, j))
    for j in range(pieces):
        core_copy(chips - 1, j).wait_recv()
        total = kept[chips - 1, j] + recv_core[chips - 1, j].astype(F32)
        for i in range(chips - 1):
            chip_copy(i, j).wait_recv()
            total = total + recv_chip[i, j].astype(F32)
        out_ref[:, j * width : (j + 1) * width] = total.astype(BF16)

    def drain(place):
        block = place * 2 + y
        for kind in (1, 0):

            @pl.when((place <= p) & has_up)
            def _():
                gather_copy(0, block, kind).wait_send()

            @pl.when((place >= p) & has_down)
            def _():
                gather_copy(1, block, kind).wait_send()

            gather_copy(2, block, kind).wait_send()

    repeat(0, line, drain)
    for i in range(chips):
        for j in range(pieces):
            core_copy(i, j).wait_send()
            if i < chips - 1:
                chip_copy(i, j).wait_send()


def solution(mesh):
    seq_count, tensor_count = mesh.shape["seq"], mesh.shape["tensor"]

    def body(queries, keys, values, out_weight, doc_lengths, stretch_place):
        rows, q_width = queries.shape
        kv_width = keys.shape[1]
        model = out_weight.shape[1]
        kv_local = kv_width // HD
        wide = q_width // kv_width * rows
        chips = tensor_count // 2
        chunk = model // tensor_count
        pieces = max(1, chunk // 256)
        width = chunk // pieces
        smem = pl.BlockSpec(memory_space=pltpu.SMEM)
        anywhere = pl.BlockSpec(memory_space=pl.ANY)
        dma = pltpu.SemaphoreType.DMA
        return pl.pallas_call(
            functools.partial(kernel, seq_count, tensor_count, pieces),
            out_shape=jax.ShapeDtypeStruct((rows, chunk), BF16),
            in_specs=[smem, smem] + [anywhere] * 4,
            out_specs=pl.BlockSpec(memory_space=pltpu.VMEM),
            scratch_shapes=[
                pltpu.VMEM((rows, q_width), BF16),
                pltpu.VMEM((rows, kv_width), BF16),
                pltpu.VMEM((seq_count, rows, kv_width), BF16),
                pltpu.VMEM((seq_count, rows, kv_width), BF16),
                pltpu.VMEM((kv_local, wide, HD), BF16),
                pltpu.VMEM((tensor_count, q_width, chunk), BF16),
                pltpu.VMEM((rows, q_width), BF16),
                pltpu.VMEM((kv_local, 1, wide), F32),
                pltpu.VMEM((kv_local, 1, wide), F32),
                pltpu.VMEM((kv_local, HD, wide), F32),
                pltpu.VMEM((chips, pieces, rows, width), F32),
                pltpu.VMEM((chips, pieces, rows, width), BF16),
                pltpu.VMEM((chips, pieces, rows, width), BF16),
                pltpu.VMEM((chips - 1, pieces, rows, width), BF16),
                pltpu.VMEM((chips - 1, pieces, rows, width), BF16),
                dma((3 + tensor_count,)),
                dma((3, seq_count // 2, 2)),
                dma((seq_count, 2)),
                dma((chips, pieces)),
                dma((chips, pieces)),
                dma((chips - 1, pieces)),
                dma((chips - 1, pieces)),
            ],
            compiler_params=pltpu.CompilerParams(collective_id=0, has_side_effects=True),
            name="attention_layer",
        )(doc_lengths, stretch_place, queries, keys, values, out_weight)

    in_specs = (
        P("seq", "tensor"),
        P("seq", "tensor"),
        P("seq", "tensor"),
        P("tensor", None),
        P(),
        P(),
    )
    return jax.shard_map(
        body, mesh=mesh, in_specs=in_specs, out_specs=P("seq", "tensor"), check_vma=False
    )
```

time: 108 us -> 32.1 us (0.30)
  waiting for transfers between devices: 38.2 us -> 0 us
  other arithmetic: 32.8 us -> 0 us
  Pallas kernels: 0 us -> 30.3 us
  between operations: 13.7 us -> 0.01 us
  starting transfers between devices: 10.4 us -> 0 us
  matrix products: 8.65 us -> 0 us
  local copies, waits for them, and re-layouts: 3.95 us -> 1.62 us
    pallas_call x0 -> x1, Pallas kernels: none -> 30.3 us  [body(): pl.pallas_call(functools.partial(kernel, seq_count, tensor_count, pieces)...]
    reduce_scatter x1 -> x0, waiting for transfers between devices: 24.5 us -> none  [body(): lax.psum_scatter(partial_rows.astype(jnp.bfloat16), 'tensor', scatter_dim...]
    ppermute x6 -> x0, waiting for transfers between devices: 13.7 us -> none  [from_partner(): return lax.ppermute(block, axis, route)]
    add x3 -> x0, other arithmetic: 11.3 us -> none  [the longest x2 11.2 us: seq_positions(): stretch_place[row_index // block_rows] * block_rows + row_index % block_rows]
    ppermute x6 -> x0, starting transfers between devices: 10.4 us -> none  [from_partner(): return lax.ppermute(block, axis, route)]
    convert_element_type x1 -> x0, other arithmetic: 9.97 us -> none  [rotary(): angles = positions.astype(jnp.float32)[:, None] * freqs[None, :]]
    gather x12 -> x0, other arithmetic: 9.07 us -> none  [seq_positions(): stretch_place[row_index // block_rows] * block_rows + row_index % block_rows]
    dot_general x9 -> x0, matrix products: 8.65 us -> none  [the longest x1 5.72 us: body(): jnp.dot(attended, out_weight, preferred_element_type=jnp.float32)]
  transfers between devices with their start and end apart: 7 -> 0, of which waited for: 4 -> 0; matrix products, arithmetic and copies ran while one was open for 23% -> 0% of each run, Pallas kernels for 0% -> 0%
where the time goes in v1:
time: 32.1 us; the launch traced here: 32 us
  Pallas kernels  30.3 us (94%)
  local copies, waits for them, and re-layouts  1.62 us (5%)
    pallas_call x1, Pallas kernels, body(): pl.pallas_call(functools.partial(kernel, seq_count, tensor_count, pieces)...  30.3 us
    unnamed x1, local copies, waits for them, and re-layouts  1.62 us

profile of v1, /device:TPU:0, one launch (start us, length us, event | category | flops | bytes accessed | tf_op | source)
XLA Modules:
  0.0 32.0 jit_solution(1446723889942646974)
XLA Ops:
  0.0 30.3 %attention_layer.1 = bf16[96,1024]{1,0:T(8,128)(2,1)} custom-call(s32[16]{0:T(128)} %lengths_ref.1, s32[16]{0:T(128)} %place_ref.1, bf16[96,1024]{1,0:T(8,128)(2,1)} %q_hbm.1, bf16[96,256]{1,0:T(8,128)(2,1)} %k_hbm.1, bf16[96,256]{1,0:T(8,128)(2,1)} %v_hbm.1, bf16[1024,4096]{1,0:T(8,128)(2,1)} %w_hbm.1), custom_call_target="tpu_custom_call" | custom-call | tf_op jit(solution)/shard_map/attention_layer/pallas_call | solution.py:370
  30.3 1.6 %copy.8 = bf16[96,1024]{1,0:T(8,128)(2,1)} copy(bf16[96,1024]{1,0:T(8,128)(2,1)} %attention_layer.1) | data formatting | bytes 393216

commit v2 on v1

--- a/solution.py
+++ b/solution.py
@@ -16,6 +16,8 @@
 BF16 = jnp.bfloat16
 MESH = pl.DeviceIdType.MESH
 UNROLL_MOST = 8
+DIRECT_MOST = 2
+VMEM_LIMIT = 50 * 1024 * 1024
 
 
 def kernel(
@@ -67,6 +69,8 @@
     t = lax.axis_index("tensor")
     a, c = t // 2, t % 2
     has_up, has_down = p < line - 1, p > 0
+    direct = 2 < line <= DIRECT_MOST
+    from_end = lambda place: (place == 0) | (place == line - 1)
     beside = p * 2 + (1 - y)
     other_core = a * 2 + (1 - c)
 
@@ -96,14 +100,34 @@
     def _():
         greet({"seq": me - 2})
 
-    pl.semaphore_wait(
-        barrier, 1 + chips + has_up.astype(jnp.int32) + has_down.astype(jnp.int32)
-    )
+    greeted = 1 + chips + has_up.astype(jnp.int32) + has_down.astype(jnp.int32)
+    if direct:
+        for apart in range(2, line):
+
+            @pl.when(p + apart < line)
+            def _():
+                @pl.when((p == 0) | (p + apart == line - 1))
+                def _():
+                    greet({"seq": me + 2 * apart})
+
+            @pl.when(p - apart >= 0)
+            def _():
+                @pl.when((p == line - 1) | (p - apart == 0))
+                def _():
+                    greet({"seq": me - 2 * apart})
+
+            above = (p + apart < line) & ((p == 0) | (p + apart == line - 1))
+            below = (p - apart >= 0) & ((p == line - 1) | (p - apart == 0))
+            greeted = greeted + above.astype(jnp.int32) + below.astype(jnp.int32)
+    pl.semaphore_wait(barrier, greeted)
+
+    def far_target(apart):
+        return me + jnp.where(p == 0, 2 * apart, -2 * apart)
 
     def gather_copy(way, block, kind, own=False):
         buf = gk if kind == 0 else gv
         src = v_hbm if own and kind == 1 else buf.at[block]
-        target = (me + 2, me - 2, beside)[way]
+        target = (me + 2, me - 2, beside)[way] if way < 3 else far_target(way - 1)
         return pltpu.make_async_remote_copy(
             src_ref=src,
             dst_ref=buf.at[block],
@@ -114,6 +138,13 @@
         )
 
     def send_own(kind):
+        if direct:
+            for apart in range(line - 1, 1, -1):
+
+                @pl.when(from_end(p))
+                def _():
+                    gather_copy(apart + 1, me, kind, True).start()
+
         @pl.when(has_up)
         def _():
             gather_copy(0, me, kind, True).start()
@@ -130,11 +161,13 @@
     def forward(place, kind):
         block = place * 2 + y
 
-        @pl.when((place < p) & has_up)
+        keep = from_end(place) if direct else place != place
+
+        @pl.when((place < p) & has_up & ~keep)
         def _():
             gather_copy(0, block, kind).start()
 
-        @pl.when((place > p) & has_down)
+        @pl.when((place > p) & has_down & ~keep)
         def _():
             gather_copy(1, block, kind).start()
 
@@ -240,16 +273,22 @@
         single = jnp.where(p < line - 1 - p, p + (k - near), p - (k - near))
         return jnp.where(k <= 2 * near, both, single)
 
+    def attend_across(k):
+        across = nth_place(k) * 2 + (1 - y)
+        for kind in (1, 0):
+            arrived(across, kind)
+        attend(across)
+
     def step(k):
         place = nth_place(k)
         for kind in (1, 0):
             arrived(place * 2 + y, kind)
             forward(place, kind)
         attend(place * 2 + y)
-        across = nth_place(k - 1) * 2 + (1 - y)
-        for kind in (1, 0):
-            arrived(across, kind)
-        attend(across)
+
+        @pl.when(k > 1)
+        def _():
+            attend_across(k - 2)
 
     def repeat(low, high, body):
         if high - low < UNROLL_MOST:
@@ -264,10 +303,8 @@
             lax.fori_loop(low, high, one, 0)
 
     repeat(1, line, step)
-    across = nth_place(jnp.int32(line - 1)) * 2 + (1 - y)
-    for kind in (1, 0):
-        arrived(across, kind)
-    attend(across)
+    for k in range(max(0, line - 2), line):
+        attend_across(jnp.int32(k))
 
     for h in range(kv_local):
         mixed = (accum[h] * (1.0 / run_total[h])).T.astype(BF16)
@@ -327,23 +364,32 @@
         for i in range(chips - 1):
             chip_copy(i, j).wait_recv()
             total = total + recv_chip[i, j].astype(F32)
-        out_ref[:, j * width : (j + 1) * width] = total.astype(BF16)
+        out_ref[:, j * width : (j + 1) * width] = total
 
     def drain(place):
         block = place * 2 + y
+        keep = from_end(place) & (place != p) if direct else place != place
         for kind in (1, 0):
 
-            @pl.when((place <= p) & has_up)
+            @pl.when((place <= p) & has_up & ~keep)
             def _():
                 gather_copy(0, block, kind).wait_send()
 
-            @pl.when((place >= p) & has_down)
+            @pl.when((place >= p) & has_down & ~keep)
             def _():
                 gather_copy(1, block, kind).wait_send()
 
             gather_copy(2, block, kind).wait_send()
 
     repeat(0, line, drain)
+    if direct:
+        for apart in range(line - 1, 1, -1):
+            for kind in (1, 0):
+
+                @pl.when(from_end(p))
+                def _():
+                    gather_copy(apart + 1, me, kind).wait_send()
+
     for i in range(chips):
         for j in range(pieces):
             core_copy(i, j).wait_send()
@@ -365,11 +411,11 @@
         pieces = max(1, chunk // 256)
         width = chunk // pieces
         smem = pl.BlockSpec(memory_space=pltpu.SMEM)
-        anywhere = pl.BlockSpec(memory_space=pl.ANY)
+        anywhere = pl.BlockSpec(memory_space=pltpu.HBM)
         dma = pltpu.SemaphoreType.DMA
-        return pl.pallas_call(
+        total = pl.pallas_call(
             functools.partial(kernel, seq_count, tensor_count, pieces),
-            out_shape=jax.ShapeDtypeStruct((rows, chunk), BF16),
+            out_shape=jax.ShapeDtypeStruct((rows, chunk), F32),
             in_specs=[smem, smem] + [anywhere] * 4,
             out_specs=pl.BlockSpec(memory_space=pltpu.VMEM),
             scratch_shapes=[
@@ -389,16 +435,22 @@
                 pltpu.VMEM((chips - 1, pieces, rows, width), BF16),
                 pltpu.VMEM((chips - 1, pieces, rows, width), BF16),
                 dma((3 + tensor_count,)),
-                dma((3, seq_count // 2, 2)),
+                dma((2 + max(1, min(seq_count // 2, DIRECT_MOST) - 1), seq_count // 2, 2)),
                 dma((seq_count, 2)),
                 dma((chips, pieces)),
                 dma((chips, pieces)),
                 dma((chips - 1, pieces)),
                 dma((chips - 1, pieces)),
             ],
-            compiler_params=pltpu.CompilerParams(collective_id=0, has_side_effects=True),
+            compiler_params=pltpu.CompilerParams(
+                collective_id=0, has_side_effects=True, vmem_limit_bytes=VMEM_LIMIT
+            ),
             name="attention_layer",
-        )(doc_lengths, stretch_place, queries, keys, values, out_weight)
+        )(*[
+            pltpu.with_memory_space_constraint(x, pltpu.HBM)
+            for x in (doc_lengths, stretch_place, queries, keys, values, out_weight)
+        ])
+        return total.astype(BF16)
 
     in_specs = (
         P("seq", "tensor"),

time: 32.1 us -> 29.9 us (0.931)
  local copies, waits for them, and re-layouts: 1.62 us -> 0 us
  Pallas kernels: 30.3 us -> 29 us
  other arithmetic: 0 us -> 0.7 us
    unnamed x1 -> x0, local copies, waits for them, and re-layouts: 1.62 us -> none
    pallas_call x1, Pallas kernels: 30.3 us -> 29 us  [body(): pl.pallas_call(functools.partial(kernel, seq_count, tensor_count, pieces)...]
    convert_element_type x0 -> x1, other arithmetic: none -> 0.7 us  [body(): return total.astype(BF16)]
where the time goes in v2:
time: 29.9 us; the launch traced here: 29.8 us
  Pallas kernels  29 us (97%)
  other arithmetic  0.7 us (2%)
    pallas_call x1, Pallas kernels, body(): pl.pallas_call(functools.partial(kernel, seq_count, tensor_count, pieces)...  29 us
    convert_element_type x1, other arithmetic, body(): return total.astype(BF16)  0.7 us

profile of v2, /device:TPU:0, one launch (start us, length us, event | category | flops | bytes accessed | tf_op | source)
XLA Modules:
  0.0 29.8 jit_solution(17310096361200220446)
XLA Ops:
  0.0 29.0 %attention_layer.1 = f32[96,1024]{1,0:T(8,128)S(1)} custom-call(s32[16]{0:T(128)} %lengths_ref.1, s32[16]{0:T(128)} %place_ref.1, bf16[96,1024]{1,0:T(8,128)(2,1)} %q_hbm.1, bf16[96,256]{1,0:T(8,128)(2,1)} %k_hbm.1, bf16[96,256]{1,0:T(8,128)(2,1)} %v_hbm.1, bf16[1024,4096]{1,0:T(8,128)(2,1)} %w_hbm.1), custom_call_target="tpu_custom_call" | custom-call | tf_op jit(solution)/shard_map/attention_layer/pallas_call | solution.py:416
  29.0 0.7 %convert_element_type.3 = bf16[96,1024]{1,0:T(8,128)(2,1)} convert(f32[96,1024]{1,0:T(8,128)S(1)} %attention_layer.1) | non-fusion elementwise | flops 98304 | bytes 589824 | tf_op jit(solution)/shard_map/convert_element_type | solution.py:453

commit v3 on v2

--- a/solution.py
+++ b/solution.py
@@ -212,6 +212,23 @@
     for load in weight_loads:
         load.start()
 
+    near = jnp.minimum(p, line - 1 - p)
+
+    def nth_place(k):
+        apart = (k + 1) // 2
+        both = jnp.where(k % 2 == 1, p - apart, p + apart)
+        single = jnp.where(p < line - 1 - p, p + (k - near), p - (k - near))
+        return jnp.where(k <= 2 * near, both, single)
+
+    def relay(k):
+        place = nth_place(k)
+        for kind in (1, 0):
+            arrived(place * 2 + y, kind)
+            forward(place, kind)
+
+    for k in range(1, min(3, line)):
+        relay(jnp.int32(k))
+
     loads[2].wait()
     for h in range(kv_local):
         for g in range(group):
@@ -265,14 +282,6 @@
     loads[1].wait()
     attend(me)
 
-    near = jnp.minimum(p, line - 1 - p)
-
-    def nth_place(k):
-        apart = (k + 1) // 2
-        both = jnp.where(k % 2 == 1, p - apart, p + apart)
-        single = jnp.where(p < line - 1 - p, p + (k - near), p - (k - near))
-        return jnp.where(k <= 2 * near, both, single)
-
     def attend_across(k):
         across = nth_place(k) * 2 + (1 - y)
         for kind in (1, 0):
@@ -280,11 +289,11 @@
         attend(across)
 
     def step(k):
-        place = nth_place(k)
-        for kind in (1, 0):
-            arrived(place * 2 + y, kind)
-            forward(place, kind)
-        attend(place * 2 + y)
+        attend(nth_place(k) * 2 + y)
+
+        @pl.when(k + 2 < line)
+        def _():
+            relay(k + 2)
 
         @pl.when(k > 1)
         def _():
@@ -408,7 +417,7 @@
         wide = q_width // kv_width * rows
         chips = tensor_count // 2
         chunk = model // tensor_count
-        pieces = max(1, chunk // 256)
+        pieces = max(1, chunk // 512)
         width = chunk // pieces
         smem = pl.BlockSpec(memory_space=pltpu.SMEM)
         anywhere = pl.BlockSpec(memory_space=pltpu.HBM)

time: 29.9 us -> 29.3 us (0.980)
  Pallas kernels: 29 us -> 28.4 us
    pallas_call x1, Pallas kernels: 29 us -> 28.4 us  [body(): pl.pallas_call(functools.partial(kernel, seq_count, tensor_count, pieces)...]
where the time goes in v3:
time: 29.3 us; the launch traced here: 29.1 us
  Pallas kernels  28.4 us (97%)
  other arithmetic  0.7 us (2%)
    pallas_call x1, Pallas kernels, body(): pl.pallas_call(functools.partial(kernel, seq_count, tensor_count, pieces)...  28.4 us
    convert_element_type x1, other arithmetic, body(): return total.astype(BF16)  0.7 us

profile of v3, /device:TPU:0, one launch (start us, length us, event | category | flops | bytes accessed | tf_op | source)
XLA Modules:
  0.0 29.1 jit_solution(16412653170987126374)
XLA Ops:
  0.0 28.4 %attention_layer.1 = f32[96,1024]{1,0:T(8,128)S(1)} custom-call(s32[16]{0:T(128)} %lengths_ref.1, s32[16]{0:T(128)} %place_ref.1, bf16[96,1024]{1,0:T(8,128)(2,1)} %q_hbm.1, bf16[96,256]{1,0:T(8,128)(2,1)} %k_hbm.1, bf16[96,256]{1,0:T(8,128)(2,1)} %v_hbm.1, bf16[1024,4096]{1,0:T(8,128)(2,1)} %w_hbm.1), custom_call_target="tpu_custom_call" | custom-call | tf_op jit(solution)/shard_map/attention_layer/pallas_call | solution.py:425
  28.4 0.7 %convert_element_type.3 = bf16[96,1024]{1,0:T(8,128)(2,1)} convert(f32[96,1024]{1,0:T(8,128)S(1)} %attention_layer.1) | non-fusion elementwise | flops 98304 | bytes 589824 | tf_op jit(solution)/shard_map/convert_element_type | solution.py:462

commit v4 on v3

--- a/solution.py
+++ b/solution.py
@@ -100,6 +100,19 @@
     def _():
         greet({"seq": me - 2})
 
+    base0 = place_ref[2 * me] * half_rows
+    base1 = place_ref[2 * me + 1] * half_rows
+
+    def positions(shape, axis):
+        row = lax.broadcasted_iota(jnp.int32, shape, axis) % rows
+        return jnp.where(row < half_rows, base0 + row, base1 + row - half_rows)
+
+    lane = lax.broadcasted_iota(jnp.int32, (rows, HD), 1)
+    freq = jnp.exp((lane % (HD // 2)).astype(F32) * (-2.0 / HD * math.log(ROPE_BASE)))
+    angle = positions((rows, HD), 0).astype(F32) * freq
+    cosine = jnp.cos(angle)
+    sine = jnp.where(lane < HD // 2, -jnp.sin(angle), jnp.sin(angle))
+
     greeted = 1 + chips + has_up.astype(jnp.int32) + has_down.astype(jnp.int32)
     if direct:
         for apart in range(2, line):
@@ -187,19 +200,6 @@
                 w_hbm.at[:, pl.ds(start, chunk)], w_buf.at[slot], load_sem.at[3 + slot]
             )
         )
-
-    base0 = place_ref[2 * me] * half_rows
-    base1 = place_ref[2 * me + 1] * half_rows
-
-    def positions(shape, axis):
-        row = lax.broadcasted_iota(jnp.int32, shape, axis) % rows
-        return jnp.where(row < half_rows, base0 + row, base1 + row - half_rows)
-
-    lane = lax.broadcasted_iota(jnp.int32, (rows, HD), 1)
-    freq = jnp.exp((lane % (HD // 2)).astype(F32) * (-2.0 / HD * math.log(ROPE_BASE)))
-    angle = positions((rows, HD), 0).astype(F32) * freq
-    cosine = jnp.cos(angle)
-    sine = jnp.where(lane < HD // 2, -jnp.sin(angle), jnp.sin(angle))
 
     def rotate(block):
         floats = block.astype(F32)

time: 29.3 us -> 29.3 us (level)
  no operation moved by 1% of the time
where the time goes in v4:
time: 29.3 us; the launch traced here: 29.1 us
  Pallas kernels  28.4 us (97%)
  other arithmetic  0.7 us (2%)
    pallas_call x1, Pallas kernels, body(): pl.pallas_call(functools.partial(kernel, seq_count, tensor_count, pieces)...  28.4 us
    convert_element_type x1, other arithmetic, body(): return total.astype(BF16)  0.7 us

profile of v4, /device:TPU:0, one launch (start us, length us, event | category | flops | bytes accessed | tf_op | source)
XLA Modules:
  0.0 29.1 jit_solution(10065945075290944213)
XLA Ops:
  0.0 28.4 %attention_layer.1 = f32[96,1024]{1,0:T(8,128)S(1)} custom-call(s32[16]{0:T(128)} %lengths_ref.1, s32[16]{0:T(128)} %place_ref.1, bf16[96,1024]{1,0:T(8,128)(2,1)} %q_hbm.1, bf16[96,256]{1,0:T(8,128)(2,1)} %k_hbm.1, bf16[96,256]{1,0:T(8,128)(2,1)} %v_hbm.1, bf16[1024,4096]{1,0:T(8,128)(2,1)} %w_hbm.1), custom_call_target="tpu_custom_call" | custom-call | tf_op jit(solution)/shard_map/attention_layer/pallas_call | solution.py:425
  28.4 0.7 %convert_element_type.3 = bf16[96,1024]{1,0:T(8,128)(2,1)} convert(f32[96,1024]{1,0:T(8,128)S(1)} %attention_layer.1) | non-fusion elementwise | flops 98304 | bytes 589824 | tf_op jit(solution)/shard_map/convert_element_type | solution.py:462
